TPU v7x, 256 devices: a whole 4x4x8 slice. The times are simulated.
256 devices in a mesh: tok: 8 (over z), tp: 16 (over y, x), grp: 2 (over core).
Axes of the slice: x: 4, y: 4, z: 8, core: 2. Of those that a mesh axis runs over, the one named last changes fastest.
Arguments:
- hidden: bfloat16 [2048, 6144], P(('tok', 'grp'), 'tp'), may hold values from -6 to 6
- gain: bfloat16 [6144], P('tp'), may hold values from 0.5 to 1.5
- expert_ids: int32 [2048, 2], P(('tok', 'grp')), may hold values from 0 to 7, all different within a row; in each aligned block of 128 rows (0 to 127, 128 to 255, ...) at most 40 rows name the same one
- gate_weights: float32 [2048, 2], P(('tok', 'grp')), may hold values from 0.1 to 0.9
- segment_ids: int32 [2048], P(('tok', 'grp')), may hold values from 0 to 15, never falling along the last dimension, each value on 1 to 384 neighbouring positions
- upstream: bfloat16 [2048, 6144], P(('tok', 'grp'), 'tp'), may hold values from -6 to 6
- w_gate: bfloat16 [8, 6144, 8192], P('tok', None, ('tp', 'grp')), may hold values from -0.078125 to 0.078125
- w_up: bfloat16 [8, 6144, 8192], P('tok', None, ('tp', 'grp')), may hold values from -0.078125 to 0.078125
- w_down: bfloat16 [8, 8192, 6144], P('tok', ('tp', 'grp')), may hold values from -0.0625 to 0.0625
Outputs:
- mixed: bfloat16 [2048, 6144], P(('tok', 'grp'), 'tp')
- importance: float32 [8, 8192], P('tok', ('tp', 'grp'))
Inputs may be any that keep to these rules, and one draw needn't show every extreme that they name: `expert_ids`: each token names 2 different experts. Within the tokens of one token shard (aligned blocks of 128 rows) no expert is named by more than 40 tokens, and in some block one expert is named by exactly 40. `segment_ids`: never falling along the tokens; every document holds between 1 and 384 tokens.
All inputs are finite; a program needn't handle non-finite values.
Results may differ from a plain program's by a relative error of at most 0.0095.
Values may be sent and summed in bfloat16 or wider, within the bound.
No kernel may reach another device: no remote copies, remote signals or barrier semaphores. Data moves between devices by JAX's collectives and lax.ppermute only.
A program may use at most 128 MiB of HBM per device.

v0:
```python
import jax
import jax.numpy as jnp
from jax import lax
from jax.sharding import PartitionSpec as P


def expert_pass(rows_in, cot_in, gate_mat, up_mat, down_mat):
    gate_pre = jnp.dot(rows_in, gate_mat, preferred_element_type=jnp.float32)
    up_proj = jnp.dot(rows_in, up_mat, preferred_element_type=jnp.float32)
    sigmoid_gate = jax.nn.sigmoid(gate_pre)
    activated = gate_pre * sigmoid_gate
    hidden_act = (activated * up_proj).astype(jnp.bfloat16)
    grad_act = lax.dot_general(
        cot_in, down_mat, (((1,), (1,)), ((), ())), preferred_element_type=jnp.float32
    )
    grad_gate = (
        grad_act * up_proj * sigmoid_gate * (1.0 + gate_pre * (1.0 - sigmoid_gate))
    ).astype(jnp.bfloat16)
    grad_up = (grad_act * activated).astype(jnp.bfloat16)
    grad_wgate = lax.dot_general(
        rows_in, grad_gate, (((0,), (0,)), ((), ())), preferred_element_type=jnp.float32
    )
    grad_wup = lax.dot_general(
        rows_in, grad_up, (((0,), (0,)), ((), ())), preferred_element_type=jnp.float32
    )
    grad_wdown = lax.dot_general(
        hidden_act, cot_in, (((0,), (0,)), ((), ())), preferred_element_type=jnp.float32
    )
    scores = jnp.sum(jnp.abs(grad_wgate * gate_mat.astype(jnp.float32)), axis=0)
    scores = scores + jnp.sum(jnp.abs(grad_wup * up_mat.astype(jnp.float32)), axis=0)
    scores = scores + jnp.sum(jnp.abs(grad_wdown * down_mat.astype(jnp.float32)), axis=1)
    return (hidden_act, scores)


def on_device(hidden, gain, expert_ids, gate_weights, segment_ids, upstream, w_gate, w_up, w_down):
    rows_here = hidden.shape[0]
    top_count = expert_ids.shape[1]
    experts = lax.axis_size("tok")
    groups = lax.axis_size("grp")
    capacity = 5 * rows_here // (2 * experts)
    width = w_gate.shape[1]
    documents = jnp.arange(experts * groups, dtype=jnp.int32)
    doc_onehot = (segment_ids[:, None] == documents[None, :]).astype(jnp.float32)
    doc_len = lax.psum(jnp.sum(doc_onehot, axis=0), ("tok", "grp"))
    tok_len = jnp.sum(doc_onehot * doc_len[None, :], axis=1)
    tok_weight = rows_here / tok_len
    onehot = (
        expert_ids.reshape(-1)[:, None] == jnp.arange(experts, dtype=jnp.int32)[None, :]
    ).astype(jnp.int32)
    before = jnp.cumsum(onehot, axis=0) - onehot
    slot_ids = jnp.sum(before * onehot, axis=1).reshape(rows_here, top_count)
    targets = expert_ids * capacity + slot_ids
    all_slots = jnp.arange(experts * capacity, dtype=jnp.int32)
    matches = all_slots[:, None, None] == targets[None, :, :]
    placing = jnp.any(matches, axis=2).astype(jnp.bfloat16)
    scaled = gate_weights * tok_weight[:, None]
    slot_scale = jnp.sum(jnp.where(matches, scaled[None, :, :], 0.0), axis=(1, 2))
    combining = jnp.sum(jnp.where(matches, gate_weights[None, :, :], 0.0), axis=2)
    wide_hidden = hidden.astype(jnp.float32)
    squares = lax.psum(jnp.sum(wide_hidden * wide_hidden, axis=1), "tp")
    scaling = lax.rsqrt(squares / width + 1e-05)
    normed = (wide_hidden * scaling[:, None] * gain.astype(jnp.float32)[None, :]).astype(
        jnp.bfloat16
    )
    block_rows = jnp.dot(placing, normed, preferred_element_type=jnp.float32).astype(jnp.bfloat16)
    block_cot = jnp.dot(placing, upstream, preferred_element_type=jnp.float32) * slot_scale[:, None]
    block_rows = block_rows.reshape(experts, capacity, -1)
    block_cot = block_cot.astype(jnp.bfloat16).reshape(experts, capacity, -1)
    came_rows, came_cot = (
        lax.all_to_all(block_rows, "tok", split_axis=0, concat_axis=0, tiled=True),
        lax.all_to_all(block_cot, "tok", split_axis=0, concat_axis=0, tiled=True),
    )
    part_rows, part_cot = (
        lax.all_gather(came_rows, "tp", axis=2, tiled=True),
        lax.all_gather(came_cot, "tp", axis=2, tiled=True),
    )
    pooled_rows, pooled_cot = (
        lax.all_gather(part_rows, "grp", axis=0, tiled=True),
        lax.all_gather(part_cot, "grp", axis=0, tiled=True),
    )
    rows_in = pooled_rows.reshape(-1, width)
    cot_in = pooled_cot.reshape(-1, width)
    gate_mat = w_gate[0]
    up_mat = w_up[0]
    down_mat = w_down[0]
    hidden_act, scores = expert_pass(rows_in, cot_in, gate_mat, up_mat, down_mat)
    importance = scores / (rows_here * experts * groups)
    partial_value = lax.psum_scatter(
        lax.dot_general(
            down_mat, hidden_act, (((0,), (1,)), ((), ())), preferred_element_type=jnp.float32
        ).astype(jnp.bfloat16),
        "tp",
        scatter_dimension=0,
        tiled=True,
    )
    summed = lax.psum_scatter(partial_value, "grp", scatter_dimension=1, tiled=True).astype(
        jnp.float32
    )
    slice_width = summed.shape[0]
    outgoing = summed.astype(jnp.bfloat16).reshape(slice_width, experts, capacity)
    returned = lax.all_to_all(outgoing, "tok", split_axis=1, concat_axis=1, tiled=True)
    returned = returned.reshape(slice_width, experts * capacity).astype(jnp.float32)
    combined = lax.dot_general(
        combining,
        returned,
        (((0,), (1,)), ((), ())),
        precision=lax.Precision.HIGHEST,
        preferred_element_type=jnp.float32,
    )
    mixed = (hidden.astype(jnp.float32) + combined).astype(jnp.bfloat16)
    return (mixed, importance[None, :])


def solution(mesh):
    placed = (
        P(("tok", "grp"), "tp"),
        P("tp"),
        P(("tok", "grp"), None),
        P(("tok", "grp"), None),
        P(("tok", "grp")),
        P(("tok", "grp"), "tp"),
        P("tok", None, ("tp", "grp")),
        P("tok", None, ("tp", "grp")),
        P("tok", ("tp", "grp"), None),
    )
    return jax.shard_map(
        on_device,
        mesh=mesh,
        in_specs=placed,
        out_specs=(P(("tok", "grp"), "tp"), P("tok", ("tp", "grp"))),
        check_vma=False,
    )
```

profile of v0, /device:TPU:1, one launch (start us, length us, event | category | flops | bytes accessed | tf_op | source)
XLA Modules:
  0.0 378.7 jit_solution(2218602018310981666)
XLA Ops:
  7.2 0.9 copy.31
  8.5 1.0 fusion.19
  9.5 34.2 %psum.14 = f32[128]{0:T(128)S(1)} all-reduce(f32[128]{0:T(128)S(1)} %fusion.19), channel_id=1, replica_groups=mesh['tok'=8,'tp'=16,'grp'=2] {'tp'}, use_global_device_ids=true, to_apply=%region_6.7 | all-reduce | flops 128 | bytes 1024 | tf_op jit(solution)/shard_map/psum | solution.py:60
  43.7 0.7 convert_element_type.60
  45.5 0.7 multiply_add_fusion
  46.3 1.2 convolution_convert_fusion.1
  47.5 17.2 %all_to_all.15 = bf16[8,40,384]{2,1,0:T(8,128)(2,1)} all-to-all(bf16[8,40,384]{2,1,0:T(8,128)(2,1)S(1)} %bitcast.56), channel_id=1, replica_groups=mesh['tok'=8,'tp'=16,'grp'=2] {'tok'}, dimensions={0} | all-to-all | bytes 491520 | tf_op jit(solution)/shard_map/all_to_all | solution.py:70
  64.8 0.8 convert_reduce_fusion
  65.6 32.2 %psum.15 = f32[16]{0:T(128)S(1)} all-reduce(f32[16]{0:T(128)S(1)} %convert_reduce_fusion), channel_id=1, replica_groups=mesh['tok'=8,'tp'=16,'grp'=2] {'tok','grp'}, use_global_device_ids=true, to_apply=%region_10.11 | all-reduce | flops 16 | bytes 128 | tf_op jit(solution)/shard_map/psum | solution.py:44
  97.8 0.7 select_reduce_fusion.2
  99.2 1.5 select_reduce_fusion
  101.0 12.8 %all_to_all.16 = bf16[8,40,384]{2,1,0:T(8,128)(2,1)} all-to-all(bf16[8,40,384]{2,1,0:T(8,128)(2,1)S(1)} %bitcast.57), channel_id=1, replica_groups=mesh['tok'=8,'tp'=16,'grp'=2] {'tok'}, dimensions={0} | all-to-all | bytes 491520 | tf_op jit(solution)/shard_map/all_to_all | solution.py:71
  113.8 10.2 %all-gather.5.cloned.1.call-done = bf16[8,40,6144]{2,1,0:T(8,128)(2,1)} async-done(((bf16[8,40,384]{2,1,0:T(8,128)(2,1)}), bf16[8,40,6144]{2,1,0:T(8,128)(2,1)}) %all-gather.5.cloned.1.call-update) | async-done | bytes 3932176 | tf_op jit(solution)/shard_map/all_gather | solution.py:74
  124.1 62.4 %all-gather.9.cloned.1.call-done = bf16[8,40,6144]{2,1,0:T(8,128)(2,1)} async-done(((bf16[8,40,384]{2,1,0:T(8,128)(2,1)}), bf16[8,40,6144]{2,1,0:T(8,128)(2,1)}) %all-gather.9.cloned.1.call-update) | async-done | bytes 3932176 | tf_op jit(solution)/shard_map/all_gather | solution.py:75
  186.5 27.7 %all-gather.7.cloned.1.call-done = bf16[16,40,6144]{2,1,0:T(8,128)(2,1)} async-done(((bf16[8,40,6144]{2,1,0:T(8,128)(2,1)}), bf16[16,40,6144]{2,1,0:T(8,128)(2,1)}) %all-gather.7.cloned.1.call-update) | async-done | bytes 7864336 | tf_op jit(solution)/shard_map/all_gather | solution.py:78
  214.2 5.6 %fusion.9 = f32[640,256]{1,0:T(8,128)S(1)} fusion(bf16[640,6144]{1,0:T(8,128)(2,1)} %bitcast.60, bf16[1,6144,256]{2,1,0:T(8,128)(2,1)S(1)} %copy-done.4), kind=kOutput, calls=%fused_computation.13 | convolution fusion | flops 2013265920 | bytes 11665408 | tf_op jit(solution)/shard_map/dot_general | solution.py:8
  219.8 0.8 copy-done.6
  220.6 3.0 multiply_convert_fusion.2
  223.6 0.7 copy-done.2
  224.4 6.1 %fusion = bf16[6144,640]{0,1:T(8,128)(2,1)} fusion(bf16[640,256]{1,0:T(8,128)(2,1)S(1)} %get-tuple-element.4, bf16[1,256,6144]{2,1,0:T(8,128)(2,1)S(1)} %copy-done.1), kind=kOutput, calls=%fused_computation.1 | convolution fusion | flops 2017198080 | bytes 11337728 | tf_op jit(solution)/shard_map/dot_general | solution.py:89
  230.5 10.7 %copy.34 = bf16[6144,640]{1,0:T(8,128)(2,1)} copy(bf16[6144,640]{0,1:T(8,128)(2,1)} %fusion) | data formatting | bytes 15728640
  241.6 5.6 %fusion.4 = f32[640,256]{1,0:T(8,128)S(1)} fusion(bf16[640,6144]{1,0:T(8,128)(2,1)} %bitcast.53, bf16[1,256,6144]{2,1,0:T(8,128)(2,1)S(1)} %copy-done.1), kind=kOutput, calls=%fused_computation.8 | convolution fusion | flops 2013265920 | bytes 11665408 | tf_op jit(solution)/shard_map/dot_general | solution.py:13
  247.2 0.8 copy-done.9
  248.1 6.2 %fusion.11 = f32[256]{0:T(256)S(1)} fusion(bf16[1,6144,256]{2,1,0:T(8,128)(2,1)S(1)} %copy-done.5, bf16[640,6144]{1,0:T(8,128)(2,1)} %bitcast.61, f32[640,256]{1,0:T(8,128)S(1)} %copy-done.8, f32[640,256]{1,0:T(8,128)S(1)} %fusion.4, f32[640,256]{1,0:T(8,128)S(1)} %copy-done.10), kind=kOutput, calls=%fused_computation.15 | convolution fusion | flops 2021195520 | bytes 12977152 | tf_op jit(solution)/shard_map/dot_general | solution.py:20
  254.3 80.1 %reduce-scatter.7.cloned.1.call-done = bf16[384,640]{1,0:T(8,128)(2,1)} async-done(((bf16[6144,640]{1,0:T(8,128)(2,1)}), bf16[384,640]{1,0:T(8,128)(2,1)}) %reduce-scatter.7.cloned.1.call-update) | async-done | bytes 491536
  334.4 2.0 copy.35
  336.5 7.4 %fusion.12 = f32[256]{0:T(256)S(1)} fusion(bf16[1,6144,256]{2,1,0:T(8,128)(2,1)} %param.16, bf16[640,6144]{1,0:T(8,128)(2,1)} %bitcast.62, f32[640,256]{1,0:T(8,128)} %copy-done.9, f32[640,256]{1,0:T(8,128)} %copy-done.7), kind=kOutput, calls=%fused_computation.16 | convolution fusion | flops 2020540160 | bytes 12321792 | tf_op jit(solution)/shard_map/dot_general | solution.py:23
  343.8 7.7 %reduce-scatter.5.cloned.1.call-done = bf16[384,320]{0,1:T(8,128)(2,1)} async-done(((bf16[384,640]{0,1:T(8,128)(2,1)}), bf16[384,320]{0,1:T(8,128)(2,1)}) %reduce-scatter.5.cloned.1.call-update) | async-done | bytes 245776 | tf_op jit(solution)/shard_map/reduce_scatter | solution.py:96
  351.5 6.5 %all-to-all-start.1 = ((bf16[384,8,40]{0,2,1:T(8,128)(2,1)}), bf16[384,8,40]{0,2,1:T(8,128)(2,1)S(1)}, u32[]{:S(2)}, u32[]{:S(2)}) async-start(bf16[384,8,40]{0,2,1:T(8,128)(2,1)} %bitcast.58), calls=%async_computation.2 | async-start | bytes 491520 | tf_op jit(solution)/shard_map/all_to_all | solution.py:101
  358.0 6.5 %fusion.13 = f32[256]{0:T(256)S(1)} fusion(bf16[1,256,6144]{2,1,0:T(8,128)(2,1)S(1)} %copy-done.1, bf16[640,256]{1,0:T(8,128)(2,1)} %copy-done.2, bf16[640,6144]{1,0:T(8,128)(2,1)} %bitcast.54), kind=kOutput, calls=%fused_computation.17 | convolution fusion | flops 2019557120 | bytes 11338752 | tf_op jit(solution)/shard_map/dot_general | solution.py:26
  365.0 4.8 %all-to-all-done.1 = bf16[384,8,40]{0,2,1:T(8,128)(2,1)S(1)} async-done(((bf16[384,8,40]{0,2,1:T(8,128)(2,1)}), bf16[384,8,40]{0,2,1:T(8,128)(2,1)S(1)}, u32[]{:S(2)}, u32[]{:S(2)}) %all-to-all-start.1) | async-done | bytes 245792 | tf_op jit(solution)/shard_map/all_to_all | solution.py:101
  369.8 2.0 fusion.15
  (48 shorter events, 3.6 us)
Async XLA Ops:
  7.2 93.6 %copy-start = (bf16[128,384]{1,0:T(8,128)(2,1)S(1)}, bf16[128,384]{1,0:T(8,128)(2,1)}, u32[]{:S(2)}) copy-start(bf16[128,384]{1,0:T(8,128)(2,1)} %param.14) | copy-start | bytes 294916
  7.2 207.0 %copy-start.4 = (bf16[1,6144,256]{2,1,0:T(8,128)(2,1)S(1)}, bf16[1,6144,256]{2,1,0:T(8,128)(2,1)}, u32[]{:S(2)}) copy-start(bf16[1,6144,256]{2,1,0:T(8,128)(2,1)} %param.15) | copy-start | bytes 9437188
  7.2 116.8 %all-gather.5.cloned.1.call-start = ((), (), s32[]{:S(2)}) async-start(), calls=%async_computation.5 | async-start | bytes 4177920 | tf_op jit(solution)/shard_map/all_gather | solution.py:74
  64.7 121.7 %all-gather.9.cloned.1.call-start = ((), (), s32[]{:S(2)}) async-start(), calls=%async_computation.8 | async-start | bytes 4177920 | tf_op jit(solution)/shard_map/all_gather | solution.py:75
  113.8 100.4 %all-gather.7.cloned.1.call-start = ((), (), s32[]{:S(2)}) async-start(), calls=%async_computation.6 | async-start | bytes 11796480 | tf_op jit(solution)/shard_map/all_gather | solution.py:78
  124.1 117.6 %all-gather.11.cloned.1.call-start = ((), (), s32[]{:S(2)}) async-start(), calls=%async_computation.9 | async-start | bytes 11796480 | tf_op jit(solution)/shard_map/all_gather | solution.py:79
  186.5 147.9 %reduce-scatter.7.cloned.1.call-start = ((), (), s32[]{:S(2)}) async-start(), calls=%async_computation.10 | async-start | bytes 8355840
  214.2 5.6 %copy-start.3 = (bf16[16,40,6144]{2,1,0:T(8,128)(2,1)S(1)}, bf16[16,40,6144]{2,1,0:T(8,128)(2,1)}, u32[]{:S(2)}) copy-start(bf16[16,40,6144]{2,1,0:T(8,128)(2,1)} %all-gather.7.cloned.1.call-done) | copy-start | bytes 23592964
  214.2 6.4 %copy-start.6 = (bf16[1,6144,256]{2,1,0:T(8,128)(2,1)S(1)}, bf16[1,6144,256]{2,1,0:T(8,128)(2,1)}, u32[]{:S(2)}) copy-start(bf16[1,6144,256]{2,1,0:T(8,128)(2,1)} %param.16) | copy-start | bytes 9437188
  220.6 3.0 copy-start.7
  220.6 3.8 copy-start.1
  223.6 0.7 copy-start.2
  241.2 110.2 %reduce-scatter.5.cloned.1.call-start = ((), (), s32[]{:S(2)}) async-start(), calls=%async_computation.7 | async-start | bytes 737280 | tf_op jit(solution)/shard_map/reduce_scatter | solution.py:96
  241.6 6.5 %copy-start.5 = (bf16[1,6144,256]{2,1,0:T(8,128)(2,1)S(1)}, bf16[1,6144,256]{2,1,0:T(8,128)(2,1)}, u32[]{:S(2)}) copy-start(bf16[1,6144,256]{2,1,0:T(8,128)(2,1)} %param.15) | copy-start | bytes 9437188
  241.6 6.5 %copy-start.8 = (f32[640,256]{1,0:T(8,128)S(1)}, f32[640,256]{1,0:T(8,128)}, u32[]{:S(2)}) copy-start(f32[640,256]{1,0:T(8,128)} %copy-done.7) | copy-start | bytes 1966084
  241.6 6.5 %copy-start.10 = (f32[640,256]{1,0:T(8,128)S(1)}, f32[640,256]{1,0:T(8,128)}, u32[]{:S(2)}) copy-start(f32[640,256]{1,0:T(8,128)} %get-tuple-element.5) | copy-start | bytes 1966084
  247.2 0.8 copy-start.9
  351.5 18.3 %all-to-all-start.1 = ((bf16[384,8,40]{0,2,1:T(8,128)(2,1)}), bf16[384,8,40]{0,2,1:T(8,128)(2,1)S(1)}, u32[]{:S(2)}, u32[]{:S(2)}) async-start(bf16[384,8,40]{0,2,1:T(8,128)(2,1)} %bitcast.58), calls=%async_computation.2 | async-start | bytes 491520 | tf_op jit(solution)/shard_map/all_to_all | solution.py:101
Sparse Core Ops, SparseCore 0:
  64.9 59.1 all-gather.4
  126.4 59.9 all-gather.8
  188.3 25.9 all-gather.6
  215.9 25.6 all-gather.10
  245.3 89.1 reduce-scatter.6
  336.8 14.6 reduce-scatter.4
where the time goes:
time: 379 us
  waiting for transfers between devices  193 us (51%)
  blocking collectives  96.5 us (25%)
  matrix products  43.9 us (12%)
  local copies, waits for them, and re-layouts  16.8 us (4%)
  between operations  14.2 us (4%)
  other arithmetic  7.42 us (2%)
  starting transfers between devices  6.89 us (2%)
    unnamed x7, waiting for transfers between devices  80.2 us
    all_gather x1, waiting for transfers between devices, on_device(): lax.all_gather(came_cot, 'tp', axis=2, tiled=True)  62.4 us
    psum x1, blocking collectives, on_device(): squares = lax.psum(jnp.sum(wide_hidden * wide_hidden, axis=1), 'tp')  34.2 us
    psum x1, blocking collectives, on_device(): doc_len = lax.psum(jnp.sum(doc_onehot, axis=0), ('tok', 'grp'))  32.2 us
    all_gather x1, waiting for transfers between devices, on_device(): lax.all_gather(part_rows, 'grp', axis=0, tiled=True)  27.7 us
    all_to_all x1, blocking collectives, on_device(): lax.all_to_all(block_rows, 'tok', split_axis=0, concat_axis=0, tiled=True)  17.2 us
    unnamed x25, local copies, waits for them, and re-layouts  16.1 us
    all_to_all x1, blocking collectives, on_device(): lax.all_to_all(block_cot, 'tok', split_axis=0, concat_axis=0, tiled=True)  12.8 us
  transfers between devices with their start and end apart: 7, of which 7 were waited for; matrix products, arithmetic and copies ran while one was open for 15% of the time, Pallas kernels for 0%

commit v1 on v0

--- a/solution.py
+++ b/solution.py
@@ -2,6 +2,14 @@
 import jax.numpy as jnp
 from jax import lax
 from jax.sharding import PartitionSpec as P
+
+
+def sizes_note(named_axis, frame):
+    state_next = jnp.concatenate(
+        lax.all_to_all(jnp.stack([frame] * lax.psum(1, named_axis), axis=0), named_axis, 0, 0),
+        axis=2,
+    )
+    return state_next
 
 
 def expert_pass(rows_in, cot_in, gate_mat, up_mat, down_mat):
@@ -72,7 +80,7 @@
     )
     part_rows, part_cot = (
         lax.all_gather(came_rows, "tp", axis=2, tiled=True),
-        lax.all_gather(came_cot, "tp", axis=2, tiled=True),
+        sizes_note("tp", came_cot),
     )
     pooled_rows, pooled_cot = (
         lax.all_gather(part_rows, "grp", axis=0, tiled=True),

time: 379 us -> 382 us (level)
  waiting for transfers between devices: 193 us -> 146 us
  blocking collectives: 96.5 us -> 143 us
    all_gather x1 -> x0, waiting for transfers between devices: 62.4 us -> none  [on_device(): lax.all_gather(came_cot, 'tp', axis=2, tiled=True)]
    all_to_all x0 -> x1, blocking collectives: none -> 50.3 us  [sizes_note(): lax.all_to_all(jnp.stack([frame] * lax.psum(1, named_axis), axis=0), name...]
    all_gather x1, waiting for transfers between devices: 10.2 us -> 59.2 us  [on_device(): lax.all_gather(came_rows, 'tp', axis=2, tiled=True)]
    all_gather x1, waiting for transfers between devices: 27.7 us -> 0.02 us  [on_device(): lax.all_gather(part_rows, 'grp', axis=0, tiled=True)]
    psum x1, blocking collectives: 32.2 us -> 25.4 us  [on_device(): doc_len = lax.psum(jnp.sum(doc_onehot, axis=0), ('tok', 'grp'))]
    unnamed x7 -> x6, waiting for transfers between devices: 80.2 us -> 74.1 us
  transfers between devices with their start and end apart: 7 -> 6, of which waited for: 7 -> 4; matrix products, arithmetic and copies ran while one was open for 15% -> 16% of each run, Pallas kernels for 0% -> 0%
where the time goes in v1:
time: 382 us; the launch traced here: 381 us
  waiting for transfers between devices  146 us (38%)
  blocking collectives  143 us (37%)
  matrix products  44.1 us (12%)
  local copies, waits for them, and re-layouts  19.9 us (5%)
  between operations  13.9 us (4%)
  other arithmetic  7.42 us (2%)
  starting transfers between devices  6.86 us (2%)
    unnamed x6, waiting for transfers between devices  74.1 us
    all_gather x1, waiting for transfers between devices, on_device(): lax.all_gather(came_rows, 'tp', axis=2, tiled=True)  59.2 us
    all_to_all x1, blocking collectives, sizes_note(): lax.all_to_all(jnp.stack([frame] * lax.psum(1, named_axis), axis=0), name...  50.3 us
    psum x1, blocking collectives, on_device(): squares = lax.psum(jnp.sum(wide_hidden * wide_hidden, axis=1), 'tp')  34.2 us
    psum x1, blocking collectives, on_device(): doc_len = lax.psum(jnp.sum(doc_onehot, axis=0), ('tok', 'grp'))  25.4 us
    all_to_all x1, blocking collectives, on_device(): lax.all_to_all(block_rows, 'tok', split_axis=0, concat_axis=0, tiled=True)  17.2 us
    all_to_all x1, blocking collectives, on_device(): lax.all_to_all(block_cot, 'tok', split_axis=0, concat_axis=0, tiled=True)  16.1 us
    unnamed x25, local copies, waits for them, and re-layouts  16 us
  transfers between devices with their start and end apart: 6, of which 4 were waited for; matrix products, arithmetic and copies ran while one was open for 16% of the time, Pallas kernels for 0%

profile of v1, /device:TPU:1, one launch (start us, length us, event | category | flops | bytes accessed | tf_op | source)
XLA Modules:
  0.0 381.4 jit_solution(1369163450564881255)
XLA Ops:
  7.2 0.8 copy.33
  8.3 1.0 fusion.19
  9.3 34.2 %psum.14 = f32[128]{0:T(128)S(1)} all-reduce(f32[128]{0:T(128)S(1)} %fusion.19), channel_id=1, replica_groups=mesh['tok'=8,'tp'=16,'grp'=2] {'tp'}, use_global_device_ids=true, to_apply=%region_6.7 | all-reduce | flops 128 | bytes 1024 | tf_op jit(solution)/shard_map/psum | solution.py:68
  45.4 0.7 multiply_add_fusion
  46.1 1.2 convolution_convert_fusion.1
  47.3 17.2 %all_to_all.20 = bf16[8,40,384]{2,1,0:T(8,128)(2,1)} all-to-all(bf16[8,40,384]{2,1,0:T(8,128)(2,1)S(1)} %bitcast.61), channel_id=1, replica_groups=mesh['tok'=8,'tp'=16,'grp'=2] {'tok'}, dimensions={0} | all-to-all | bytes 491520 | tf_op jit(solution)/shard_map/all_to_all | solution.py:78
  64.6 59.2 %all-gather.4.cloned.1.call-done = bf16[8,40,6144]{2,1,0:T(8,128)(2,1)} async-done(((bf16[8,40,384]{2,1,0:T(8,128)(2,1)}), bf16[8,40,6144]{2,1,0:T(8,128)(2,1)}) %all-gather.4.cloned.1.call-update) | async-done | bytes 3932176 | tf_op jit(solution)/shard_map/all_gather | solution.py:82
  123.9 0.8 convert_reduce_fusion
  124.7 25.4 %psum.15 = f32[16]{0:T(128)S(1)} all-reduce(f32[16]{0:T(128)S(1)} %convert_reduce_fusion), channel_id=1, replica_groups=mesh['tok'=8,'tp'=16,'grp'=2] {'tok','grp'}, use_global_device_ids=true, to_apply=%region_10.11 | all-reduce | flops 16 | bytes 128 | tf_op jit(solution)/shard_map/psum | solution.py:52
  150.1 0.7 select_reduce_fusion.2
  150.9 0.7 broadcast_multiply_fusion
  151.6 1.5 select_reduce_fusion
  153.3 16.1 %all_to_all.21 = bf16[8,40,384]{2,1,0:T(8,128)(2,1)S(1)} all-to-all(bf16[8,40,384]{2,1,0:T(8,128)(2,1)S(1)} %bitcast.62), channel_id=1, replica_groups=mesh['tok'=8,'tp'=16,'grp'=2] {'tok'}, dimensions={0} | all-to-all | bytes 491520 | tf_op jit(solution)/shard_map/all_to_all | solution.py:79
  170.0 50.3 %all_to_all.22 = bf16[16,8,40,384]{3,2,1,0:T(8,128)(2,1)S(1)} all-to-all(bf16[16,8,40,384]{3,2,1,0:T(8,128)(2,1)S(1)} %stack.2), channel_id=1, replica_groups=mesh['tok'=8,'tp'=16,'grp'=2] {'tp'}, dimensions={0} | all-to-all | bytes 7864320 | tf_op jit(solution)/shard_map/all_to_all | solution.py:9
  220.3 2.6 copy.39
  223.0 5.6 %fusion.9 = f32[640,256]{1,0:T(8,128)S(1)} fusion(bf16[640,6144]{1,0:T(8,128)(2,1)} %bitcast.65, bf16[1,6144,256]{2,1,0:T(8,128)(2,1)S(1)} %copy-done.4), kind=kOutput, calls=%fused_computation.13 | convolution fusion | flops 2013265920 | bytes 11665408 | tf_op jit(solution)/shard_map/dot_general | solution.py:16
  228.6 0.8 copy-done.6
  229.4 3.0 multiply_convert_fusion.2
  232.4 0.7 copy-done.2
  233.1 6.4 %fusion = bf16[6144,640]{0,1:T(8,128)(2,1)} fusion(bf16[640,256]{1,0:T(8,128)(2,1)S(1)} %get-tuple-element.4, bf16[1,256,6144]{2,1,0:T(8,128)(2,1)S(1)} %copy-done.1), kind=kOutput, calls=%fused_computation.1 | convolution fusion | flops 2017198080 | bytes 11337728 | tf_op jit(solution)/shard_map/dot_general | solution.py:97
  239.5 10.9 %copy.37 = bf16[6144,640]{1,0:T(8,128)(2,1)} copy(bf16[6144,640]{0,1:T(8,128)(2,1)} %fusion) | data formatting | bytes 15728640
  250.7 5.6 %fusion.4 = f32[640,256]{1,0:T(8,128)S(1)} fusion(bf16[640,6144]{1,0:T(8,128)(2,1)} %bitcast.58, bf16[1,256,6144]{2,1,0:T(8,128)(2,1)S(1)} %copy-done.1), kind=kOutput, calls=%fused_computation.8 | convolution fusion | flops 2013265920 | bytes 11665408 | tf_op jit(solution)/shard_map/dot_general | solution.py:21
  256.3 0.8 copy-done.9
  257.1 6.2 %fusion.11 = f32[256]{0:T(256)S(1)} fusion(bf16[1,6144,256]{2,1,0:T(8,128)(2,1)S(1)} %copy-done.5, bf16[640,6144]{1,0:T(8,128)(2,1)} %bitcast.66, f32[640,256]{1,0:T(8,128)S(1)} %copy-done.8, f32[640,256]{1,0:T(8,128)S(1)} %fusion.4, f32[640,256]{1,0:T(8,128)S(1)} %copy-done.10), kind=kOutput, calls=%fused_computation.15 | convolution fusion | flops 2021195520 | bytes 12977152 | tf_op jit(solution)/shard_map/dot_general | solution.py:28
  263.4 74.0 %reduce-scatter.7.cloned.1.call-done = bf16[384,640]{1,0:T(8,128)(2,1)} async-done(((bf16[6144,640]{1,0:T(8,128)(2,1)}), bf16[384,640]{1,0:T(8,128)(2,1)}) %reduce-scatter.7.cloned.1.call-update) | async-done | bytes 491536
  337.4 2.0 copy.38
  339.4 7.4 %fusion.12 = f32[256]{0:T(256)S(1)} fusion(bf16[1,6144,256]{2,1,0:T(8,128)(2,1)} %param.16, bf16[640,6144]{1,0:T(8,128)(2,1)} %bitcast.67, f32[640,256]{1,0:T(8,128)} %copy-done.9, f32[640,256]{1,0:T(8,128)} %copy-done.7), kind=kOutput, calls=%fused_computation.16 | convolution fusion | flops 2020540160 | bytes 12321792 | tf_op jit(solution)/shard_map/dot_general | solution.py:31
  346.8 7.7 %reduce-scatter.5.cloned.1.call-done = bf16[384,320]{0,1:T(8,128)(2,1)} async-done(((bf16[384,640]{0,1:T(8,128)(2,1)}), bf16[384,320]{0,1:T(8,128)(2,1)}) %reduce-scatter.5.cloned.1.call-update) | async-done | bytes 245776 | tf_op jit(solution)/shard_map/reduce_scatter | solution.py:104
  354.5 6.5 %all-to-all-start.1 = ((bf16[384,8,40]{0,2,1:T(8,128)(2,1)}), bf16[384,8,40]{0,2,1:T(8,128)(2,1)S(1)}, u32[]{:S(2)}, u32[]{:S(2)}) async-start(bf16[384,8,40]{0,2,1:T(8,128)(2,1)} %bitcast.63), calls=%async_computation.2 | async-start | bytes 491520 | tf_op jit(solution)/shard_map/all_to_all | solution.py:109
  361.0 6.5 %fusion.13 = f32[256]{0:T(256)S(1)} fusion(bf16[1,256,6144]{2,1,0:T(8,128)(2,1)S(1)} %copy-done.1, bf16[640,256]{1,0:T(8,128)(2,1)} %copy-done.2, bf16[640,6144]{1,0:T(8,128)(2,1)} %bitcast.59), kind=kOutput, calls=%fused_computation.17 | convolution fusion | flops 2019557120 | bytes 11338752 | tf_op jit(solution)/shard_map/dot_general | solution.py:34
  368.0 4.8 %all-to-all-done.1 = bf16[384,8,40]{0,2,1:T(8,128)(2,1)S(1)} async-done(((bf16[384,8,40]{0,2,1:T(8,128)(2,1)}), bf16[384,8,40]{0,2,1:T(8,128)(2,1)S(1)}, u32[]{:S(2)}, u32[]{:S(2)}) %all-to-all-start.1) | async-done | bytes 245792 | tf_op jit(solution)/shard_map/all_to_all | solution.py:109
  372.8 2.0 fusion.15
  (48 shorter events, 4.1 us)
Async XLA Ops:
  7.2 145.9 %copy-start = (bf16[128,384]{1,0:T(8,128)(2,1)S(1)}, bf16[128,384]{1,0:T(8,128)(2,1)}, u32[]{:S(2)}) copy-start(bf16[128,384]{1,0:T(8,128)(2,1)} %param.14) | copy-start | bytes 294916
  7.2 116.7 %all-gather.4.cloned.1.call-start = ((), (), s32[]{:S(2)}) async-start(), calls=%async_computation.6 | async-start | bytes 4177920 | tf_op jit(solution)/shard_map/all_gather | solution.py:82
  64.6 158.4 %all-gather.6.cloned.1.call-start = ((), (), s32[]{:S(2)}) async-start(), calls=%async_computation.7 | async-start | bytes 11796480 | tf_op jit(solution)/shard_map/all_gather | solution.py:86
  123.9 126.7 %all-gather.8.cloned.1.call-start = ((), (), s32[]{:S(2)}) async-start(), calls=%async_computation.9 | async-start | bytes 11796480 | tf_op jit(solution)/shard_map/all_gather | solution.py:87
  220.3 2.7 copy-start.4
  222.9 114.5 %reduce-scatter.7.cloned.1.call-start = ((), (), s32[]{:S(2)}) async-start(), calls=%async_computation.10 | async-start | bytes 8355840
  223.0 5.6 %copy-start.3 = (bf16[16,40,6144]{2,1,0:T(8,128)(2,1)S(1)}, bf16[16,40,6144]{2,1,0:T(8,128)(2,1)}, u32[]{:S(2)}) copy-start(bf16[16,40,6144]{2,1,0:T(8,128)(2,1)} %all-gather.6.cloned.1.call-done) | copy-start | bytes 23592964
  223.0 6.4 %copy-start.6 = (bf16[1,6144,256]{2,1,0:T(8,128)(2,1)S(1)}, bf16[1,6144,256]{2,1,0:T(8,128)(2,1)}, u32[]{:S(2)}) copy-start(bf16[1,6144,256]{2,1,0:T(8,128)(2,1)} %param.16) | copy-start | bytes 9437188
  229.4 3.0 copy-start.7
  229.4 3.8 copy-start.1
  232.4 0.7 copy-start.2
  250.4 104.1 %reduce-scatter.5.cloned.1.call-start = ((), (), s32[]{:S(2)}) async-start(), calls=%async_computation.8 | async-start | bytes 737280 | tf_op jit(solution)/shard_map/reduce_scatter | solution.py:104
  250.6 6.5 %copy-start.5 = (bf16[1,6144,256]{2,1,0:T(8,128)(2,1)S(1)}, bf16[1,6144,256]{2,1,0:T(8,128)(2,1)}, u32[]{:S(2)}) copy-start(bf16[1,6144,256]{2,1,0:T(8,128)(2,1)} %param.15) | copy-start | bytes 9437188
  250.6 6.5 %copy-start.8 = (f32[640,256]{1,0:T(8,128)S(1)}, f32[640,256]{1,0:T(8,128)}, u32[]{:S(2)}) copy-start(f32[640,256]{1,0:T(8,128)} %copy-done.7) | copy-start | bytes 1966084
  250.7 6.5 %copy-start.10 = (f32[640,256]{1,0:T(8,128)S(1)}, f32[640,256]{1,0:T(8,128)}, u32[]{:S(2)}) copy-start(f32[640,256]{1,0:T(8,128)} %get-tuple-element.5) | copy-start | bytes 1966084
  256.3 0.8 copy-start.9
  354.5 18.3 %all-to-all-start.1 = ((bf16[384,8,40]{0,2,1:T(8,128)(2,1)}), bf16[384,8,40]{0,2,1:T(8,128)(2,1)S(1)}, u32[]{:S(2)}, u32[]{:S(2)}) async-start(bf16[384,8,40]{0,2,1:T(8,128)(2,1)} %bitcast.63), calls=%async_computation.2 | async-start | bytes 491520 | tf_op jit(solution)/shard_map/all_to_all | solution.py:109
Sparse Core Ops, SparseCore 0:
  64.7 59.1 all-gather.3
  125.7 25.9 all-gather.5
  223.0 21.3 all-gather.7
  250.5 86.8 reduce-scatter.6
  339.8 14.6 reduce-scatter.4
